TPU v7x, 32 devices: a whole 2x2x4 slice. The times are simulated.
32 devices in a mesh: groups: 2 (over x), blk: 8 (over z, y), split: 2 (over core).
Axes of the slice: x: 2, y: 2, z: 4, core: 2. Of those that a mesh axis runs over, the one named last changes fastest.
Arguments:
- embeddings: bfloat16 [32768, 768], P(('groups', 'blk', 'split')), parts along dimension 0, may hold values from -6 to 6
- cluster_of: int32 [32768], P(('groups', 'blk', 'split')), parts along dimension 0, may hold values from 0 to 15, as said below
- target_pos: int32 [32768], P(('groups', 'blk', 'split')), parts along dimension 0, may hold values from 0 to 16383, as said below
Outputs:
- best: float32 [32768], P(('groups', 'blk', 'split')), parts along dimension 0
There are 2 independent parts, one for each index of `groups`. A program takes and returns all parts, laid end to end along the dimension named above; each array names one. Nothing has to cross between parts.
Inputs may be any that keep to these rules, and one draw needn't show every extreme that they name: `cluster_of`: ordering the members by target_pos lists cluster 0 first, then cluster 1 and so on, each cluster's members contiguous; every cluster has 2 to 4096 members and one has exactly 4096. `target_pos`: A permutation of the rows. For every aligned block of 1024 positions, each device's 1024 data-order rows hold exactly 64 of its positions.
All inputs are finite; a program needn't handle non-finite values.
Results may differ from a plain program's by a relative error of at most 0.0025.
Values may be sent and summed in bfloat16 or wider, within the bound.
A program may use at most 64 MiB of HBM per device.

v0:
```python
import jax
import jax.numpy as jnp
from jax import lax
from jax.sharding import PartitionSpec as P

MOST = 4096


FILL = -4.0


def from_behind(block, axis, distance):
    devices = range(lax.axis_size(axis))
    route = [((i - distance) % len(devices), i) for i in devices]
    return lax.ppermute(block, axis, route)


def masked_scores(left, left_ids, right, right_ids):
    sims = lax.dot_general(
        left, right, (((1,), (1,)), ((), ())), preferred_element_type=jnp.float32
    )
    return jnp.where(left_ids[:, None] == right_ids[None, :], sims, FILL)


def body(embeddings, cluster_of, target_pos):
    count = lax.axis_size(("blk", "split"))
    rows, width = embeddings.shape
    piece = rows // count
    me = lax.axis_index(("blk", "split"))
    values = embeddings.astype(jnp.float32)
    unit = (values * lax.rsqrt(jnp.sum(values * values, axis=1, keepdims=True) + 1e-06)).astype(
        jnp.bfloat16
    )
    order = jnp.argsort(target_pos)
    packed = unit[order].reshape(count, piece, width)
    labels = jnp.stack(
        [cluster_of[order].reshape(count, piece), target_pos[order].reshape(count, piece)], axis=1
    )
    received, tags = (
        lax.all_to_all(packed, ("blk", "split"), split_axis=0, concat_axis=0, tiled=True),
        lax.all_to_all(labels, ("blk", "split"), split_axis=0, concat_axis=0, tiled=True),
    )
    unit_in = received.reshape(rows, width)
    ids_in = tags[:, 0, :].reshape(rows)
    local = tags[:, 1, :].reshape(rows) - me * rows
    place = jnp.argsort(local)
    mine = unit_in[place]
    my_ids = ids_in[place]
    reach = (MOST + rows - 2) // rows
    own = masked_scores(mine, my_ids, mine, my_ids)
    diagonal = jnp.arange(rows)[:, None] == jnp.arange(rows)[None, :]
    best = jnp.max(jnp.where(diagonal, FILL, own), axis=1)

    def both_maxima(pair, visit_unit, visit_ids):
        row_best, visit_best = pair
        scores = masked_scores(mine, my_ids, visit_unit, visit_ids)
        return (
            jnp.maximum(row_best, jnp.max(scores, axis=1)),
            jnp.maximum(visit_best, jnp.max(scores, axis=0)),
        )

    def turn(step, carry):
        row_best, visit_unit, visit_ids, visit_best = carry
        visit_unit, visit_ids, visit_best = (
            from_behind(visit_unit, ("blk", "split"), 1),
            from_behind(visit_ids, ("blk", "split"), 1),
            from_behind(visit_best.astype(jnp.bfloat16), ("blk", "split"), 1).astype(
                visit_best.dtype
            ),
        )
        row_best, visit_best = both_maxima((row_best, visit_best), visit_unit, visit_ids)
        return (row_best, visit_unit, visit_ids, visit_best)

    start_best = jnp.full((rows,), FILL, jnp.float32)
    best, visit_unit, visit_ids, visit_best = lax.fori_loop(
        0, reach, turn, (best, mine, my_ids, start_best)
    )
    returned_home = from_behind(visit_best, ("blk", "split"), -reach)
    best = jnp.maximum(best, returned_home)
    back = best[local].reshape(count, piece)
    returned = lax.all_to_all(
        back, ("blk", "split"), split_axis=0, concat_axis=0, tiled=True
    ).reshape(rows)
    return jnp.zeros((rows,), jnp.float32).at[order].set(returned)


def solution(mesh):
    return jax.shard_map(
        body,
        mesh=mesh,
        in_specs=(
            P(("groups", "blk", "split"), None),
            P(("groups", "blk", "split")),
            P(("groups", "blk", "split")),
        ),
        out_specs=P(("groups", "blk", "split")),
        check_vma=False,
    )
```

profile of v0, /device:TPU:0, one launch (start us, length us, event | category | flops | bytes accessed | tf_op | source)
XLA Modules:
  0.0 204.1 jit_solution(9965459332306292172)
XLA Ops:
  0.0 5.1 %sort.31 = (s32[1024]{0:T(1024)}, s32[1024]{0:T(1024)S(1)}) sort(s32[1024]{0:T(1024)} %param.7, s32[1024]{0:T(1024)S(1)} %iota.15), dimensions={0}, to_apply=%region_0.0 | sort | flops 10240 | bytes 16384 | tf_op jit(solution)/shard_map/jit(argsort)/sort | solution.py:34
  5.1 4.5 %gather_fusion.1 = s32[1024]{0:T(1024)S(1)} fusion(s32[1024]{0:T(1024)S(1)} %copy-done.1, s32[1024]{0:T(1024)S(1)} %get-tuple-element.92), kind=kCustom, calls=%fused_computation.1 | custom fusion | bytes 12288 | tf_op jit(solution)/shard_map/gather | solution.py:37
  9.7 0.1 stack_reshape.7
  9.8 4.5 %gather_fusion = s32[1024]{0:T(1024)S(1)} fusion(s32[1024]{0:T(1024)S(1)} %copy-done, s32[1024]{0:T(1024)S(1)} %get-tuple-element.92), kind=kCustom, calls=%fused_computation | custom fusion | bytes 12288 | tf_op jit(solution)/shard_map/gather | solution.py:37
  14.3 0.1 stack_reshape.6
  14.4 0.7 reshape.140
  15.1 7.4 %all-to-all-start = ((s32[16,1,128]{2,1,0:T(1,128)}), s32[16,1,128]{2,1,0:T(1,128)S(1)}, u32[]{:S(2)}, u32[]{:S(2)}) async-start(s32[16,1,128]{2,1,0:T(1,128)} %reshape.140), calls=%async_computation | async-start | bytes 16384 | tf_op jit(solution)/shard_map/all_to_all | solution.py:41
  22.5 0.4 fusion.2
  22.9 0.3 fusion.3
  23.2 5.2 %gather_fusion.3 = bf16[1024,768]{1,0:T(8,128)(2,1)} fusion(bf16[1024,768]{1,0:T(8,128)(2,1)S(1)} %fusion.3, s32[1024]{0:T(1024)S(1)} %get-tuple-element.92), kind=kCustom, calls=%fused_computation.3 | custom fusion | bytes 3149824 | tf_op jit(solution)/shard_map/gather | solution.py:35
  28.4 0.5 all-to-all-done
  28.9 5.5 %all-to-all-start.1 = ((bf16[16,64,768]{2,1,0:T(8,128)(2,1)}), bf16[16,64,768]{2,1,0:T(8,128)(2,1)S(1)}, u32[]{:S(2)}, u32[]{:S(2)}) async-start(bf16[16,64,768]{2,1,0:T(8,128)(2,1)} %bitcast), calls=%async_computation.1 | async-start | bytes 3145728 | tf_op jit(solution)/shard_map/all_to_all | solution.py:40
  34.5 0.5 broadcast.95
  35.0 0.7 reduce.15
  35.7 0.1 reshape.141
  35.8 0.5 broadcast.93
  36.3 0.7 fusion.7
  37.0 0.1 sub.21
  37.0 0.1 sub.22
  37.1 0.1 reshape_squeeze.4
  37.2 4.4 %sort.32 = (s32[1024]{0:T(1024)}, s32[1024]{0:T(1024)S(1)}) sort(s32[1024]{0:T(1024)S(1)} %sub.21, s32[1024]{0:T(1024)S(1)} %iota.16), dimensions={0}, to_apply=%region_1.0 | sort | flops 10240 | bytes 16384 | tf_op jit(solution)/shard_map/jit(argsort)/sort | solution.py:46
  41.6 4.5 %gather_fusion.2 = s32[1024]{0:T(1024)S(1)} fusion(s32[1024]{0:T(1024)S(1)} %reshape_squeeze.4, s32[1024]{0:T(1024)S(1)} %fusion.4), kind=kCustom, calls=%fused_computation.2 | custom fusion | bytes 12288 | tf_op jit(solution)/shard_map/gather | solution.py:48
  46.1 20.2 %all-to-all-done.1 = bf16[16,64,768]{2,1,0:T(8,128)(2,1)S(1)} async-done(((bf16[16,64,768]{2,1,0:T(8,128)(2,1)}), bf16[16,64,768]{2,1,0:T(8,128)(2,1)S(1)}, u32[]{:S(2)}, u32[]{:S(2)}) %all-to-all-start.1) | async-done | bytes 1572896 | tf_op jit(solution)/shard_map/all_to_all | solution.py:40
  66.3 4.0 %gather_fusion.4 = bf16[1024,768]{1,0:T(8,128)(2,1)S(1)} fusion(bf16[1024,768]{1,0:T(8,128)(2,1)S(1)} %bitcast.13, s32[1024]{0:T(1024)S(1)} %fusion.4), kind=kCustom, calls=%fused_computation.4 | custom fusion | bytes 3149824 | tf_op jit(solution)/shard_map/gather | solution.py:47
  70.3 1.8 select_reduce_fusion
  72.1 1.2 copy.6
  73.3 107.0 %while.17 = (s32[]{:T(128)}, f32[1024]{0:T(1024)S(1)}, bf16[1024,768]{1,0:T(8,128)(2,1)}, s32[1024]{0:T(1024)S(1)}, f32[1024]{0:T(1024)S(1)}, /*index=5*/s32[102...) while((s32[]{:T(128)}, f32[1024]{0:T(1024)S(1)}, bf16[1024,768]{1,0:T(8,128)(2,1)}, ...), condition=%wide.region_7.8_spmd.clone, body=%wide.region_4.0_spmd.clone.sunk | while | flops 1614809088 | bytes 12660959 | solution.py:75
  73.3 1.0 collective-permute-start.1
  74.3 1.8 collective-permute-start
  76.1 1.0 collective-permute-start.2
  77.1 22.3 %collective-permute-done = s32[1024]{0:T(1024)S(1)} collective-permute-done((s32[1024]{0:T(1024)S(1)}, s32[1024]{0:T(1024)S(1)}, u32[]{:S(2)}, u32[]{:S(2)}) %collective-permute-start) | collective-permute-done | bytes 4128 | tf_op jit(solution)/shard_map/while/body/eval_jaxpr/ppermute | solution.py:15
  99.4 0.0 collective-permute-done.1
  99.4 1.9 fusion.17
  101.3 1.2 copy.16
  102.5 0.0 collective-permute-done.2
  102.5 0.0 collective-permute-start.1
  102.5 0.1 collective-permute-start
  102.6 0.1 collective-permute-start.2
  102.7 22.6 %collective-permute-done = s32[1024]{0:T(1024)S(1)} collective-permute-done((s32[1024]{0:T(1024)S(1)}, s32[1024]{0:T(1024)S(1)}, u32[]{:S(2)}, u32[]{:S(2)}) %collective-permute-start) | collective-permute-done | bytes 4128 | tf_op jit(solution)/shard_map/while/body/eval_jaxpr/ppermute | solution.py:15
  125.3 1.9 fusion.17
  127.2 1.2 copy.16
  128.4 0.0 collective-permute-start.1
  128.4 0.1 collective-permute-start
  128.5 0.1 collective-permute-start.2
  128.6 22.6 %collective-permute-done = s32[1024]{0:T(1024)S(1)} collective-permute-done((s32[1024]{0:T(1024)S(1)}, s32[1024]{0:T(1024)S(1)}, u32[]{:S(2)}, u32[]{:S(2)}) %collective-permute-start) | collective-permute-done | bytes 4128 | tf_op jit(solution)/shard_map/while/body/eval_jaxpr/ppermute | solution.py:15
  151.2 0.0 collective-permute-done.1
  151.2 1.9 fusion.17
  153.1 1.2 copy.16
  154.3 0.0 collective-permute-start.1
  154.3 0.1 collective-permute-start
  154.4 0.1 collective-permute-start.2
  154.5 22.7 %collective-permute-done = s32[1024]{0:T(1024)S(1)} collective-permute-done((s32[1024]{0:T(1024)S(1)}, s32[1024]{0:T(1024)S(1)}, u32[]{:S(2)}, u32[]{:S(2)}) %collective-permute-start) | collective-permute-done | bytes 4128 | tf_op jit(solution)/shard_map/while/body/eval_jaxpr/ppermute | solution.py:15
  177.2 0.0 collective-permute-done.1
  177.2 1.9 fusion.17
  179.2 1.2 copy.16
  180.3 0.0 collective-permute-done.2
  180.3 3.6 %collective-permute-done.3 = f32[1024]{0:T(1024)S(1)} collective-permute-done((f32[1024]{0:T(1024)S(1)}, f32[1024]{0:T(1024)S(1)}, u32[]{:S(2)}, u32[]{:S(2)}) %collective-permute-start.3) | collective-permute-done | bytes 4128 | tf_op jit(solution)/shard_map/ppermute | solution.py:15
  183.9 4.5 %gather_fusion.5 = f32[1024]{0:T(1024)S(1)} fusion(f32[1024]{0:T(1024)S(1)} %max.9, s32[1024]{0:T(1024)S(1)} %broadcast_clamp_fusion), kind=kCustom, calls=%fused_computation.5 | custom fusion | bytes 12288 | tf_op jit(solution)/shard_map/gather | solution.py:80
  188.5 0.1 all_to_all.14
  188.5 9.4 %all_to_all.19 = f32[16,1,64]{2,1,0:T(1,128)S(1)} all-to-all(f32[16,1,64]{2,1,0:T(1,128)S(1)} %all_to_all.14), channel_id=1, replica_groups=mesh['groups'=2,'blk'=8,'split'=2] {'blk','split'}, dimensions={0} | all-to-all | bytes 8192 | tf_op jit(solution)/shard_map/all_to_all | solution.py:81
  197.9 0.5 broadcast.94
  198.5 0.7 reduce.13
  199.1 0.1 reshape.102
  199.2 4.9 %scatter_custom_fusion = f32[1024]{0:T(1024)} fusion(s32[1024]{0:T(1024)S(1)} %get-tuple-element.93, f32[1024]{0:T(1024)S(1)} %reshape.102, f32[]{:T(128)} %constant.3.clone.1), kind=kCustom, calls=%fused_computation.28 | custom fusion | bytes 4100 | tf_op jit(solution)/shard_map/scatter | solution.py:84
  (37 shorter events, 0.2 us)
Async XLA Ops:
  0.0 9.8 %copy-start = (s32[1024]{0:T(1024)S(1)}, s32[1024]{0:T(1024)}, u32[]{:S(2)}) copy-start(s32[1024]{0:T(1024)} %param.6) | copy-start | bytes 12292
  0.0 5.1 %copy-start.1 = (s32[1024]{0:T(1024)S(1)}, s32[1024]{0:T(1024)}, u32[]{:S(2)}) copy-start(s32[1024]{0:T(1024)} %param.7) | copy-start | bytes 12292
  9.8 12.7 %copy-start.2 = (bf16[1024,768]{1,0:T(8,128)(2,1)S(1)}, bf16[1024,768]{1,0:T(8,128)(2,1)}, u32[]{:S(2)}) copy-start(bf16[1024,768]{1,0:T(8,128)(2,1)} %param.5) | copy-start | bytes 4718596
  15.1 13.8 %all-to-all-start = ((s32[16,1,128]{2,1,0:T(1,128)}), s32[16,1,128]{2,1,0:T(1,128)S(1)}, u32[]{:S(2)}, u32[]{:S(2)}) async-start(s32[16,1,128]{2,1,0:T(1,128)} %reshape.140), calls=%async_computation | async-start | bytes 16384 | tf_op jit(solution)/shard_map/all_to_all | solution.py:41
  28.9 37.4 %all-to-all-start.1 = ((bf16[16,64,768]{2,1,0:T(8,128)(2,1)}), bf16[16,64,768]{2,1,0:T(8,128)(2,1)S(1)}, u32[]{:S(2)}, u32[]{:S(2)}) async-start(bf16[16,64,768]{2,1,0:T(8,128)(2,1)} %bitcast), calls=%async_computation.1 | async-start | bytes 3145728 | tf_op jit(solution)/shard_map/all_to_all | solution.py:40
  73.3 26.1 %collective-permute-start.1 = (bf16[1024,768]{1,0:T(8,128)(2,1)}, bf16[1024,768]{1,0:T(8,128)(2,1)S(1)}, u32[]{:S(2)}, u32[]{:S(2)}) collective-permute-start(bf16[1024,768]{1,0:T(8,128)(2,1)} %get-tuple-element.152), channel_id=1, source_target_pairs={{15,0},{0,1},{1,2},{2,3},{3,4},{4,5},{5,6},{6,7},{7,8},{8,9},{9,10... | collective-permute-start | bytes 4718600 | tf_op jit(solution)/shard_map/while/body/eval_jaxpr/ppermute | solution.py:15
  74.3 25.1 %collective-permute-start = (s32[1024]{0:T(1024)S(1)}, s32[1024]{0:T(1024)S(1)}, u32[]{:S(2)}, u32[]{:S(2)}) collective-permute-start(s32[1024]{0:T(1024)S(1)} %get-tuple-element.153), channel_id=1, source_target_pairs={{15,0},{0,1},{1,2},{2,3},{3,4},{4,5},{5,6},{6,7},{7,8},{8,9},{9,10... | collective-permute-start | bytes 12296 | tf_op jit(solution)/shard_map/while/body/eval_jaxpr/ppermute | solution.py:15
  76.1 26.4 %collective-permute-start.2 = (bf16[1024]{0:T(1024)(128)(2,1)S(1)}, bf16[1024]{0:T(1024)(128)(2,1)S(1)}, u32[]{:S(2)}, u32[]{:S(2)}) collective-permute-start(bf16[1024]{0:T(1024)(128)(2,1)S(1)} %select_convert_fusion.2), channel_id=1, source_target_pairs={{15,0},{0,1},{1,2},{2,3},{3,4},{4,5},{5,6},{6,7},{7,8},{8,9},{9,10... | collective-permute-start | bytes 6152 | tf_op jit(solution)/shard_map/while/body/eval_jaxpr/ppermute | solution.py:15
  102.5 22.8 %collective-permute-start.1 = (bf16[1024,768]{1,0:T(8,128)(2,1)}, bf16[1024,768]{1,0:T(8,128)(2,1)S(1)}, u32[]{:S(2)}, u32[]{:S(2)}) collective-permute-start(bf16[1024,768]{1,0:T(8,128)(2,1)} %get-tuple-element.152), channel_id=1, source_target_pairs={{15,0},{0,1},{1,2},{2,3},{3,4},{4,5},{5,6},{6,7},{7,8},{8,9},{9,10... | collective-permute-start | bytes 4718600 | tf_op jit(solution)/shard_map/while/body/eval_jaxpr/ppermute | solution.py:15
  102.5 22.8 %collective-permute-start = (s32[1024]{0:T(1024)S(1)}, s32[1024]{0:T(1024)S(1)}, u32[]{:S(2)}, u32[]{:S(2)}) collective-permute-start(s32[1024]{0:T(1024)S(1)} %get-tuple-element.153), channel_id=1, source_target_pairs={{15,0},{0,1},{1,2},{2,3},{3,4},{4,5},{5,6},{6,7},{7,8},{8,9},{9,10... | collective-permute-start | bytes 12296 | tf_op jit(solution)/shard_map/while/body/eval_jaxpr/ppermute | solution.py:15
  102.6 25.8 %collective-permute-start.2 = (bf16[1024]{0:T(1024)(128)(2,1)S(1)}, bf16[1024]{0:T(1024)(128)(2,1)S(1)}, u32[]{:S(2)}, u32[]{:S(2)}) collective-permute-start(bf16[1024]{0:T(1024)(128)(2,1)S(1)} %select_convert_fusion.2), channel_id=1, source_target_pairs={{15,0},{0,1},{1,2},{2,3},{3,4},{4,5},{5,6},{6,7},{7,8},{8,9},{9,10... | collective-permute-start | bytes 6152 | tf_op jit(solution)/shard_map/while/body/eval_jaxpr/ppermute | solution.py:15
  128.4 22.8 %collective-permute-start.1 = (bf16[1024,768]{1,0:T(8,128)(2,1)}, bf16[1024,768]{1,0:T(8,128)(2,1)S(1)}, u32[]{:S(2)}, u32[]{:S(2)}) collective-permute-start(bf16[1024,768]{1,0:T(8,128)(2,1)} %get-tuple-element.152), channel_id=1, source_target_pairs={{15,0},{0,1},{1,2},{2,3},{3,4},{4,5},{5,6},{6,7},{7,8},{8,9},{9,10... | collective-permute-start | bytes 4718600 | tf_op jit(solution)/shard_map/while/body/eval_jaxpr/ppermute | solution.py:15
  128.4 22.8 %collective-permute-start = (s32[1024]{0:T(1024)S(1)}, s32[1024]{0:T(1024)S(1)}, u32[]{:S(2)}, u32[]{:S(2)}) collective-permute-start(s32[1024]{0:T(1024)S(1)} %get-tuple-element.153), channel_id=1, source_target_pairs={{15,0},{0,1},{1,2},{2,3},{3,4},{4,5},{5,6},{6,7},{7,8},{8,9},{9,10... | collective-permute-start | bytes 12296 | tf_op jit(solution)/shard_map/while/body/eval_jaxpr/ppermute | solution.py:15
  128.5 25.8 %collective-permute-start.2 = (bf16[1024]{0:T(1024)(128)(2,1)S(1)}, bf16[1024]{0:T(1024)(128)(2,1)S(1)}, u32[]{:S(2)}, u32[]{:S(2)}) collective-permute-start(bf16[1024]{0:T(1024)(128)(2,1)S(1)} %select_convert_fusion.2), channel_id=1, source_target_pairs={{15,0},{0,1},{1,2},{2,3},{3,4},{4,5},{5,6},{6,7},{7,8},{8,9},{9,10... | collective-permute-start | bytes 6152 | tf_op jit(solution)/shard_map/while/body/eval_jaxpr/ppermute | solution.py:15
  154.3 22.9 %collective-permute-start.1 = (bf16[1024,768]{1,0:T(8,128)(2,1)}, bf16[1024,768]{1,0:T(8,128)(2,1)S(1)}, u32[]{:S(2)}, u32[]{:S(2)}) collective-permute-start(bf16[1024,768]{1,0:T(8,128)(2,1)} %get-tuple-element.152), channel_id=1, source_target_pairs={{15,0},{0,1},{1,2},{2,3},{3,4},{4,5},{5,6},{6,7},{7,8},{8,9},{9,10... | collective-permute-start | bytes 4718600 | tf_op jit(solution)/shard_map/while/body/eval_jaxpr/ppermute | solution.py:15
  154.3 22.9 %collective-permute-start = (s32[1024]{0:T(1024)S(1)}, s32[1024]{0:T(1024)S(1)}, u32[]{:S(2)}, u32[]{:S(2)}) collective-permute-start(s32[1024]{0:T(1024)S(1)} %get-tuple-element.153), channel_id=1, source_target_pairs={{15,0},{0,1},{1,2},{2,3},{3,4},{4,5},{5,6},{6,7},{7,8},{8,9},{9,10... | collective-permute-start | bytes 12296 | tf_op jit(solution)/shard_map/while/body/eval_jaxpr/ppermute | solution.py:15
  154.4 25.9 %collective-permute-start.2 = (bf16[1024]{0:T(1024)(128)(2,1)S(1)}, bf16[1024]{0:T(1024)(128)(2,1)S(1)}, u32[]{:S(2)}, u32[]{:S(2)}) collective-permute-start(bf16[1024]{0:T(1024)(128)(2,1)S(1)} %select_convert_fusion.2), channel_id=1, source_target_pairs={{15,0},{0,1},{1,2},{2,3},{3,4},{4,5},{5,6},{6,7},{7,8},{8,9},{9,10... | collective-permute-start | bytes 6152 | tf_op jit(solution)/shard_map/while/body/eval_jaxpr/ppermute | solution.py:15
  180.3 3.6 %collective-permute-start.3 = (f32[1024]{0:T(1024)S(1)}, f32[1024]{0:T(1024)S(1)}, u32[]{:S(2)}, u32[]{:S(2)}) collective-permute-start(f32[1024]{0:T(1024)S(1)} %get-tuple-element.48), channel_id=1, source_target_pairs={{4,0},{5,1},{6,2},{7,3},{8,4},{9,5},{10,6},{11,7},{12,8},{13,9},{1... | collective-permute-start | bytes 12296 | tf_op jit(solution)/shard_map/ppermute | solution.py:15
where the time goes:
time: 204 us
  waiting for transfers between devices  115 us (56%)
  local copies, waits for them, and re-layouts  40.8 us (20%)
  starting transfers between devices  17.1 us (8%)
  other arithmetic  12.3 us (6%)
  matrix products  9.56 us (5%)
  blocking collectives  9.41 us (5%)
    ppermute x13, waiting for transfers between devices, from_behind(): return lax.ppermute(block, axis, route)  93.9 us
    all_to_all x1, waiting for transfers between devices, body(): lax.all_to_all(packed, ('blk', 'split'), split_axis=0, concat_axis=0, til...  20.2 us
    dot_general x5, matrix products, masked_scores(): lax.dot_general(left, right, (((1,), (1,)), ((), ())), preferred_element_...  9.56 us
    all_to_all x1, blocking collectives, body(): lax.all_to_all(back, ('blk', 'split'), split_axis=0, concat_axis=0, tiled...  9.41 us
    all_to_all x1, starting transfers between devices, body(): lax.all_to_all(labels, ('blk', 'split'), split_axis=0, concat_axis=0, til...  7.41 us
    all_to_all x1, starting transfers between devices, body(): lax.all_to_all(packed, ('blk', 'split'), split_axis=0, concat_axis=0, til...  5.53 us
    gather x1, local copies, waits for them, and re-layouts, body(): packed = unit[order].reshape(count, piece, width)  5.21 us
    sort x1, other arithmetic, body(): order = jnp.argsort(target_pos)  5.12 us
  transfers between devices with their start and end apart: 15, of which 7 were waited for; matrix products, arithmetic and copies ran while one was open for 15% of the time, Pallas kernels for 0%

commit v1 on v0

v1 whole, which is shorter than its diff:
```python
import functools

import jax
import jax.numpy as jnp
from jax import lax
from jax.experimental import pallas as pl
from jax.experimental.pallas import tpu as pltpu
from jax.sharding import PartitionSpec as P

MOST = 4096
FILL = -4.0
MESH = pl.DeviceIdType.MESH
F32 = jnp.float32
BF16 = jnp.bfloat16


def nt(a, b):
    return lax.dot_general(a, b, (((1,), (1,)), ((), ())), preferred_element_type=F32)


def pack_kernel(n, emb, cl, tp, packed, idm, key_ref):
    rows, width = emb.shape
    piece = rows // n
    nq, cr = n // 4, 2 * piece
    shift = rows.bit_length() - 1
    x = emb[...].astype(F32)
    unit = (x * lax.rsqrt(jnp.sum(x * x, axis=1, keepdims=True) + 1e-06)).astype(BF16)
    dest = lax.shift_right_logical(tp[...], shift)
    hit = lax.broadcasted_iota(jnp.int32, (n, rows), 0) == dest
    hot = jnp.where(hit, 1.0, 0.0)
    i0 = lax.broadcasted_iota(jnp.int32, (rows, rows), 0)
    i1 = lax.broadcasted_iota(jnp.int32, (rows, rows), 1)
    before = jnp.where(i0 < i1, 1.0, 0.0).astype(BF16)
    counts = jnp.dot(hot.astype(BF16), before, preferred_element_type=F32)
    rank = jnp.sum(hot * counts, axis=0, keepdims=True).astype(jnp.int32)
    key = dest * piece + rank
    key_ref[...] = key
    perm = jnp.where(i0 == key, 1.0, 0.0).astype(BF16)
    zero = jnp.zeros((cr, width), BF16)
    packed[pl.ds(0, cr), :] = zero
    packed[pl.ds(cr, rows), :] = jnp.dot(perm, unit, preferred_element_type=F32).astype(BF16)
    packed[pl.ds(cr + rows, cr), :] = zero
    labels = jnp.broadcast_to(cl[...].astype(F32), (8, rows)).astype(BF16)
    ids = nt(labels, perm).astype(jnp.int32)[0:1]
    none = jnp.full((1, cr), -1, jnp.int32)
    padded = jnp.concatenate([none, ids, none], axis=1)
    for q in range(nq):
        idm[q, 0:1, :] = padded[:, 2 * cr * q : 2 * cr * (q + 1)]
        idm[q, 1:2, :] = padded[:, 2 * cr * (q + 1) : 2 * cr * (q + 2)]
        idm[q, 2:3, :] = ids[:, 2 * cr * q : 2 * cr * (q + 1)]
        idm[q, 3:8, :] = jnp.zeros((5, 2 * cr), jnp.int32)


def pick(table, hot):
    hi = table.astype(BF16)
    rest = table - hi.astype(F32)
    mid = rest.astype(BF16)
    low = (rest - mid.astype(F32)).astype(BF16)
    out = jnp.dot(hi, hot, preferred_element_type=F32)
    out += jnp.dot(mid, hot, preferred_element_type=F32)
    return out + jnp.dot(low, hot, preferred_element_type=F32)


def main_kernel(
    n, packed, idm, key_ref, out_ref,
    A, Q, IDS, MSG, MSGR, racc, cacc, colid, qid,
    init_s, recv, relay_s, y_s, y_r, c_s, c_r, d_s, d_r, loc, self_sem, ids_s, ids_r, msg_s, msg_r,
):
    nq = n // 4
    cr2 = packed.shape[1]
    cr = cr2 // 2
    rows = nq * cr2
    blk, split = lax.axis_index("blk"), lax.axis_index("split")
    me = blk * 2 + split
    q = blk // 2
    r = lax.rem(blk, 2) * 2 + split

    def dev(index):
        return {"blk": index // 2, "split": lax.rem(index, 2)}

    core = 4 * q + lax.rem(blk, 2) * 2 + (1 - split)
    across = 4 * q + lax.rem(r + 2, 4)
    rc = lax.rem(blk, 2) * 2 + (1 - split)
    ry = lax.rem(r + 2, 4)
    rd = lax.rem(rc + 2, 4)

    barrier = pltpu.get_barrier_semaphore()

    @pl.loop(1, n)
    def _(o):
        pl.semaphore_signal(
            barrier, inc=1, device_id=dev(lax.rem(me + o, n)), device_id_type=MESH
        )

    pl.semaphore_wait(barrier, n - 1)

    def remote(src, dst, s_sem, r_sem, index):
        return pltpu.make_async_remote_copy(
            src_ref=src, dst_ref=dst, send_sem=s_sem, recv_sem=r_sem,
            device_id=dev(index), device_id_type=MESH,
        )

    def ids_copy(o):
        to = lax.rem(me + o, n)
        return remote(idm.at[to // 4], IDS.at[me], ids_s.at[o], ids_r.at[me], to)

    def ids_in(o):
        frm = lax.rem(me + o, n)
        return remote(idm.at[0], IDS.at[frm], ids_s.at[o], ids_r.at[frm], frm)

    @pl.loop(1, n)
    def _(o):
        ids_copy(o).start()

    EDGE = {0: pl.ds(cr, cr), nq: pl.ds(0, cr)}

    def init(g):
        if g == 0:
            return q != 0, remote(
                packed.at[0, EDGE[0]], A.at[0, q, EDGE[0]], init_s.at[g], recv.at[0, q], r
            )
        if g == nq:
            return q != nq - 1, remote(
                packed.at[nq, EDGE[nq]], A.at[1, q, EDGE[nq]], init_s.at[g], recv.at[1, q],
                4 * (nq - 1) + r,
            )
        low = jnp.logical_or(q < g - 1, q == g)
        target = jnp.where(low, g - 1, g)
        side = g - target
        return None, remote(
            packed.at[g], A.at[side, q], init_s.at[g], recv.at[side, q], 4 * target + r
        )

    def when(cond, do):
        if cond is None:
            do()
        else:
            pl.when(cond)(do)

    for g in range(nq + 1):
        cond, copy = init(g)
        when(cond, copy.start)

    selfs = [pltpu.make_async_copy(packed.at[q + k], A.at[k, q], self_sem.at[k]) for k in (0, 1)]
    for copy in selfs:
        copy.start()

    @pl.loop(1, n)
    def _(o):
        ids_in(o).wait_recv()

    IDS[me] = idm[q]

    half = (pl.ds(cr, cr), pl.ds(0, cr))
    home = (pl.ds(0, cr), pl.ds(cr, cr))

    def parts(k, s):
        mine = A.at[k, s, half[k]]
        y = remote(mine, Q.at[r, s, home[k]], y_s.at[k, s], y_r.at[k, s], across)
        c = remote(mine, Q.at[r, s, home[k]], c_s.at[k, s], c_r.at[k, s], core)
        own = pltpu.make_async_copy(mine, Q.at[r, s, home[k]], loc.at[k, s])
        return y, c, own

    def forward(k, s):
        for copy in parts(k, s):
            copy.start()

    def y_in(k, s):
        return remote(A.at[k, s, half[k]], Q.at[ry, s, home[k]], y_s.at[k, s], y_r.at[k, s], across)

    def diag(k, s):
        there = Q.at[ry, s, home[k]]
        return remote(there, there, d_s.at[k, s], d_r.at[k, s], core)

    def diag_forward(k, s):
        y_in(k, s).wait_recv()
        diag(k, s).start()

    def c_in(k, s):
        return remote(A.at[k, s, half[k]], Q.at[rc, s, home[k]], c_s.at[k, s], c_r.at[k, s], core)

    def d_in(k, s):
        there = Q.at[rd, s, home[k]]
        return remote(there, there, d_s.at[k, s], d_r.at[k, s], core)

    def arrived(k, s, part=None):
        dst = A.at[k, s] if part is None else A.at[k, s, part]
        src = packed.at[0] if part is None else packed.at[0, part]
        remote(src, dst, relay_s.at[k, s], recv.at[k, s], me).wait_recv()

    def relay(k, s):
        to = me + 4 if k == 1 else me - 4
        return remote(A.at[k, s], A.at[1 - k, s], relay_s.at[k, s], recv.at[1 - k, s], to)

    last = {0: q == 0, 1: q == nq - 1}

    def first_stop(k, s):
        @pl.when(last[k])
        def _():
            arrived(k, s, half[k])

        @pl.when(jnp.logical_not(last[k]))
        def _():
            arrived(k, s)
            relay(k, s).start()

        forward(k, s)

    def second_stop(k, s):
        arrived(k, s)
        forward(k, s)

    def source(kind, k, d):
        below = (kind == "first") == (k == 1)
        s = q - d if below else q + d
        return s, (s >= 0 if below else s < nq)

    items = []
    order = [("first", 1), ("second", 1)]
    order += [("first", d) for d in range(2, nq)] + [("second", d) for d in range(2, nq)]
    for kind, d in order:
        for k in (1, 0):
            items.append((kind, k, d))

    for copy in selfs:
        copy.wait()
    for k in (0, 1):
        forward(k, q)

    def diag_item(item):
        kind, k, d = item
        s, ok = source(kind, k, d)

        @pl.when(ok)
        def _():
            diag_forward(k, s)

    lag = 4
    for t, (kind, k, d) in enumerate(items):
        s, ok = source(kind, k, d)

        @pl.when(ok)
        def _(kind=kind, k=k, s=s):
            (first_stop if kind == "first" else second_stop)(k, s)

        if t == 1:
            for kk in (0, 1):
                diag_forward(kk, q)
        if t >= lag:
            diag_item(items[t - lag])
    for item in items[max(0, len(items) - lag):]:
        diag_item(item)

    for p in range(4):
        qid[p, 0:1, :] = jnp.concatenate([IDS[4 * s + p, 2:3, :] for s in range(nq)], axis=1)
    row = jnp.concatenate([IDS[4 * s + r, k : k + 1, :] for k in (0, 1) for s in range(nq)], axis=1)
    colid[...] = jnp.broadcast_to(row, (128, 2 * rows)).T.reshape(colid.shape)
    racc[...] = jnp.full(racc.shape, FILL, F32)
    cacc[...] = jnp.full(cacc.shape, FILL, F32)

    @pl.loop(0, nq)
    def _(s):
        for k in (0, 1):
            parts(k, s)[2].wait()
            c_in(k, s).wait_recv()
            d_in(k, s).wait_recv()

    lane = lax.broadcasted_iota(jnp.int32, (cr2, 128), 1)
    sub = lax.broadcasted_iota(jnp.int32, (cr2, 128), 0)

    @pl.loop(0, 8 * nq)
    def _(step):
        p = step // (2 * nq)
        ks = lax.rem(step, 2 * nq)
        k, s = ks // nq, lax.rem(ks, nq)
        right = Q[p].reshape(rows, Q.shape[-1])
        scores = nt(A[k, s], right)
        col = colid[ks]
        own = jnp.where(k == 0, jnp.where(sub >= cr, 1, 0), jnp.where(sub < cr, 1, 0))
        own = jnp.where(p == r, own, 0)
        twin = jnp.where(own == 1, s * cr2 + sub + jnp.where(k == 0, -cr, cr), -1) - lane
        acc = racc[ks]
        for j in range(rows // 128):
            at = slice(128 * j, 128 * (j + 1))
            keep = jnp.logical_and(col == qid[p, 0:1, at], twin != 128 * j)
            block = jnp.where(keep, scores[:, at], FILL)
            acc = jnp.maximum(acc, block)
            cacc[p, 0:1, at] = jnp.maximum(cacc[p, 0:1, at], jnp.max(block, axis=0, keepdims=True))
        racc[ks] = acc

    best = jnp.max(racc[...].reshape(2 * rows, 128).T, axis=0, keepdims=True)
    fill = jnp.full((1, cr2), FILL, F32)
    for s in range(nq):
        for p in range(4):
            to = 4 * s + p
            same = p == r
            for k in (0, 1):
                at = (k * nq + s) * cr2
                MSG[to, k : k + 1, :] = jnp.where(same, best[:, at : at + cr2], fill)
            MSG[to, 2:3, :] = cacc[p, 0:1, cr2 * s : cr2 * (s + 1)]
            MSG[to, 3:8, :] = jnp.zeros((5, cr2), F32)

    def msg_copy(o):
        to = lax.rem(me + o, n)
        return remote(MSG.at[to], MSGR.at[me], msg_s.at[o], msg_r.at[me], to)

    @pl.loop(1, n)
    def _(o):
        msg_copy(o).start()

    MSGR[me] = MSG[me]

    for g in range(nq + 1):
        cond, copy = init(g)
        when(cond, copy.wait_send)

    @pl.loop(1, n)
    def _(o):
        ids_copy(o).wait_send()

    @pl.loop(0, nq)
    def _(s):
        for k in (0, 1):
            y, c, _ = parts(k, s)
            y.wait_send()
            c.wait_send()
            diag(k, s).wait_send()

    for kind, k, d in items:
        if kind == "first":
            s, ok = source(kind, k, d)

            @pl.when(jnp.logical_and(ok, jnp.logical_not(last[k])))
            def _(k=k, s=s):
                relay(k, s).wait_send()

    key = key_ref[...]
    bits = cr2.bit_length() - 1
    i0 = lax.broadcasted_iota(jnp.int32, (cr2, rows), 0)
    hot_q = jnp.where(i0 == (key & (cr2 - 1)), 1.0, 0.0).astype(BF16)
    hot_s = jnp.where(i0 == ((key + cr) & (cr2 - 1)), 1.0, 0.0).astype(BF16)
    at_q = lax.shift_right_logical(key, bits)
    at_s = lax.shift_right_logical(key + cr, bits)

    @pl.loop(1, n)
    def _(o):
        frm = lax.rem(me + o, n)
        remote(MSG.at[0], MSGR.at[frm], msg_s.at[o], msg_r.at[frm], frm).wait_recv()

    def top(s, k):
        found = MSGR[4 * s, k : k + 1, :]
        for p in range(1, 4):
            found = jnp.maximum(found, MSGR[4 * s + p, k : k + 1, :])
        return found

    segs = []
    for g in range(nq + 1):
        if g == 0:
            segs.append(top(0, 0))
        elif g == nq:
            segs.append(top(nq - 1, 1))
        else:
            segs.append(jnp.maximum(top(g, 0), top(g - 1, 1)))
    quads = [top(s, 2) for s in range(nq)]
    pad = -(-(nq + 1) // 8) * 8
    table_s = jnp.concatenate(segs + [fill] * (pad - nq - 1), axis=0)
    table_q = jnp.concatenate(quads + [fill] * (pad - nq), axis=0)
    which = lax.broadcasted_iota(jnp.int32, (pad, rows), 0)
    from_s = jnp.where(which == at_s, pick(table_s, hot_s), FILL)
    from_q = jnp.where(which == at_q, pick(table_q, hot_q), FILL)
    out_ref[...] = jnp.max(jnp.maximum(from_s, from_q), axis=0, keepdims=True)

    @pl.loop(1, n)
    def _(o):
        msg_copy(o).wait_send()


def body(n, embeddings, cluster_of, target_pos):
    rows, width = embeddings.shape
    piece = rows // n
    nq, cr = n // 4, 2 * piece
    assert MOST <= 4 * rows and n % 4 == 0
    vmem = pl.BlockSpec(memory_space=pltpu.VMEM)
    packed, idm, key = pl.pallas_call(
        functools.partial(pack_kernel, n),
        out_shape=(
            jax.ShapeDtypeStruct((rows + 2 * cr, width), BF16),
            jax.ShapeDtypeStruct((nq, 8, 2 * cr), jnp.int32),
            jax.ShapeDtypeStruct((1, rows), jnp.int32),
        ),
        in_specs=[vmem] * 3,
        out_specs=(vmem,) * 3,
        compiler_params=pltpu.CompilerParams(vmem_limit_bytes=40 * 2**20),
    )(embeddings, cluster_of.reshape(1, rows), target_pos.reshape(1, rows))
    dma = pltpu.SemaphoreType.DMA
    out = pl.pallas_call(
        functools.partial(main_kernel, n),
        out_shape=jax.ShapeDtypeStruct((1, rows), F32),
        in_specs=[vmem] * 3,
        out_specs=vmem,
        scratch_shapes=[
            pltpu.VMEM((2, nq, 2 * cr, width), BF16),
            pltpu.VMEM((4, nq, 2 * cr, width), BF16),
            pltpu.VMEM((n, 8, 2 * cr), jnp.int32),
            pltpu.VMEM((n, 8, 2 * cr), F32),
            pltpu.VMEM((n, 8, 2 * cr), F32),
            pltpu.VMEM((2 * nq, 2 * cr, 128), F32),
            pltpu.VMEM((4, 8, rows), F32),
            pltpu.VMEM((2 * nq, 2 * cr, 128), jnp.int32),
            pltpu.VMEM((4, 8, rows), jnp.int32),
            dma((nq + 1,)),
            dma((2, nq)), dma((2, nq)), dma((2, nq)), dma((2, nq)),
            dma((2, nq)), dma((2, nq)), dma((2, nq)), dma((2, nq)),
            dma((2, nq)), dma((2,)), dma((n,)), dma((n,)), dma((n,)), dma((n,)),
        ],
        compiler_params=pltpu.CompilerParams(
            collective_id=0, has_side_effects=True, vmem_limit_bytes=48 * 2**20
        ),
    )(packed.reshape(nq + 1, 2 * cr, width), idm, key)
    return out.reshape(rows)


def solution(mesh):
    n = mesh.shape["blk"] * mesh.shape["split"]
    spec = P(("groups", "blk", "split"))
    return jax.shard_map(
        functools.partial(body, n),
        mesh=mesh,
        in_specs=(P(("groups", "blk", "split"), None), spec, spec),
        out_specs=spec,
        check_vma=False,
    )
```

time: 204 us -> 98.5 us (0.48)
  waiting for transfers between devices: 115 us -> 0 us
  Pallas kernels: 0 us -> 94.8 us
  local copies, waits for them, and re-layouts: 40.8 us -> 3.38 us
  starting transfers between devices: 17.1 us -> 0 us
  other arithmetic: 12.3 us -> 0 us
  matrix products: 9.56 us -> 0 us
  blocking collectives: 9.41 us -> 0 us
    pallas_call x0 -> x2, Pallas kernels: none -> 94.8 us  [the longest x1 92.1 us: body(): pl.pallas_call(functools.partial(main_kernel, n), out_shape=jax.ShapeDtyp...]
    ppermute x13 -> x0, waiting for transfers between devices: 93.9 us -> none  [from_behind(): return lax.ppermute(block, axis, route)]
    gather x6 -> x0, local copies, waits for them, and re-layouts: 27.3 us -> none  [the longest x1 5.21 us: body(): packed = unit[order].reshape(count, piece, width)]
    all_to_all x2 -> x0, waiting for transfers between devices: 20.7 us -> none  [the longest x1 20.2 us: body(): lax.all_to_all(packed, ('blk', 'split'), split_axis=0, concat_axis=0, til...]
    all_to_all x2 -> x0, starting transfers between devices: 12.9 us -> none  [the longest x1 7.41 us: body(): lax.all_to_all(labels, ('blk', 'split'), split_axis=0, concat_axis=0, til...]
    dot_general x5 -> x0, matrix products: 9.56 us -> none  [masked_scores(): lax.dot_general(left, right, (((1,), (1,)), ((), ())), preferred_element_...]
    sort x2 -> x0, other arithmetic: 9.49 us -> none  [the longest x1 5.12 us: body(): order = jnp.argsort(target_pos)]
    all_to_all x1 -> x0, blocking collectives: 9.41 us -> none  [body(): lax.all_to_all(back, ('blk', 'split'), split_axis=0, concat_axis=0, tiled...]
  transfers between devices with their start and end apart: 15 -> 0, of which waited for: 7 -> 0; matrix products, arithmetic and copies ran while one was open for 15% -> 0% of each run, Pallas kernels for 0% -> 0%
where the time goes in v1:
time: 98.5 us; the launch traced here: 98.2 us
  Pallas kernels  94.8 us (96%)
  local copies, waits for them, and re-layouts  3.38 us (3%)
    pallas_call x1, Pallas kernels, body(): pl.pallas_call(functools.partial(main_kernel, n), out_shape=jax.ShapeDtyp...  92.1 us
    unnamed x7, local copies, waits for them, and re-layouts  3.38 us
    pallas_call x1, Pallas kernels, body(): pl.pallas_call(functools.partial(pack_kernel, n), out_shape=(jax.ShapeDty...  2.72 us

profile of v1, /device:TPU:0, one launch (start us, length us, event | category | flops | bytes accessed | tf_op | source)
XLA Modules:
  0.0 98.2 jit_solution(16764918912354311720)
XLA Ops:
  0.0 0.0 copy-start
  0.0 1.4 %copy-done = bf16[1024,768]{1,0:T(8,128)(2,1)S(1)} copy-done((bf16[1024,768]{1,0:T(8,128)(2,1)S(1)}, bf16[1024,768]{1,0:T(8,128)(2,1)}, u32[]{:S(2)}) %copy-start) | copy-done | bytes 1572888
  1.4 0.0 copy-start.1
  1.4 0.7 copy-done.1
  2.1 0.0 copy-start.2
  2.1 0.7 copy-done.2
  2.8 2.7 %shard_map.37 = (bf16[1280,768]{1,0:T(8,128)(2,1)S(1)}, s32[4,8,256]{2,1,0:T(8,128)S(1)}, s32[1,1024]{1,0:T(1,128)S(1)}) custom-call(bf16[1024,768]{1,0:T(8,128)(2,1)S(1)} %copy-done, s32[1,1024]{1,0:T(1,128)S(1)} %bitcast.6, s32[1,1024]{1,0:T(1,128)S(1)} %bitcast.7), custom_call_target="tpu_custom_call" | custom-call | tf_op jit(solution)/shard_map/pallas_call | solution.py:384
  5.5 92.1 %shard_map.38 = f32[1,1024]{1,0:T(1,128)S(1)} custom-call(bf16[5,256,768]{2,1,0:T(8,128)(2,1)S(1)} %bitcast.4, s32[4,8,256]{2,1,0:T(8,128)S(1)} %get-tuple-element.9.idm, s32[1,1024]{1,0:T(1,128)S(1)} %get-tuple-element.10.key_ref), custom_call_target="tpu_custom_call" | custom-call | tf_op jit(solution)/shard_map/pallas_call | solution.py:396
  97.6 0.6 copy.5
Async XLA Ops:
  0.0 1.4 %copy-start = (bf16[1024,768]{1,0:T(8,128)(2,1)S(1)}, bf16[1024,768]{1,0:T(8,128)(2,1)}, u32[]{:S(2)}) copy-start(bf16[1024,768]{1,0:T(8,128)(2,1)} %emb.1) | copy-start | bytes 4718596
  1.4 0.7 copy-start.1
  2.1 0.7 copy-start.2

commit v2 on v1

--- a/solution.py
+++ b/solution.py
@@ -137,9 +137,16 @@
         else:
             pl.when(cond)(do)
 
-    for g in range(nq + 1):
-        cond, copy = init(g)
-        when(cond, copy.start)
+    def start_if(cond, g):
+        pl.when(cond)(init(g)[1].start)
+
+    for i in range(1, nq):
+        start_if(q < nq - i - 1, nq - i)
+        start_if(q > i, i)
+    start_if(q != nq - 1, nq)
+    start_if(q != 0, 0)
+    for g in range(1, nq):
+        start_if(jnp.logical_or(q == g, q == g - 1), g)
 
     selfs = [pltpu.make_async_copy(packed.at[q + k], A.at[k, q], self_sem.at[k]) for k in (0, 1)]
     for copy in selfs:
@@ -151,142 +158,149 @@
 
     IDS[me] = idm[q]
 
-    half = (pl.ds(cr, cr), pl.ds(0, cr))
-    home = (pl.ds(0, cr), pl.ds(cr, cr))
-
-    def parts(k, s):
-        mine = A.at[k, s, half[k]]
-        y = remote(mine, Q.at[r, s, home[k]], y_s.at[k, s], y_r.at[k, s], across)
-        c = remote(mine, Q.at[r, s, home[k]], c_s.at[k, s], c_r.at[k, s], core)
-        own = pltpu.make_async_copy(mine, Q.at[r, s, home[k]], loc.at[k, s])
-        return y, c, own
+    def half(k):
+        return pl.ds(pl.multiple_of(cr * (1 - k), cr), cr)
+
+    def mine(k, s):
+        return A.at[k, s, half(k)]
+
+    def y_copy(k, s):
+        return remote(mine(k, s), Q.at[s, k, r], y_s.at[k, s], y_r.at[k, s], across)
+
+    def c_copy(k, s):
+        return remote(mine(k, s), Q.at[s, k, r], c_s.at[k, s], c_r.at[k, s], core)
+
+    def own_copy(k, s):
+        return pltpu.make_async_copy(mine(k, s), Q.at[s, k, r], loc.at[k, s])
 
     def forward(k, s):
-        for copy in parts(k, s):
-            copy.start()
+        y_copy(k, s).start()
+        c_copy(k, s).start()
+        own_copy(k, s).start()
 
     def y_in(k, s):
-        return remote(A.at[k, s, half[k]], Q.at[ry, s, home[k]], y_s.at[k, s], y_r.at[k, s], across)
+        return remote(mine(k, s), Q.at[s, k, ry], y_s.at[k, s], y_r.at[k, s], across)
 
     def diag(k, s):
-        there = Q.at[ry, s, home[k]]
+        there = Q.at[s, k, ry]
         return remote(there, there, d_s.at[k, s], d_r.at[k, s], core)
 
-    def diag_forward(k, s):
-        y_in(k, s).wait_recv()
-        diag(k, s).start()
-
     def c_in(k, s):
-        return remote(A.at[k, s, half[k]], Q.at[rc, s, home[k]], c_s.at[k, s], c_r.at[k, s], core)
+        return remote(mine(k, s), Q.at[s, k, rc], c_s.at[k, s], c_r.at[k, s], core)
 
     def d_in(k, s):
-        there = Q.at[rd, s, home[k]]
+        there = Q.at[s, k, rd]
         return remote(there, there, d_s.at[k, s], d_r.at[k, s], core)
 
-    def arrived(k, s, part=None):
-        dst = A.at[k, s] if part is None else A.at[k, s, part]
-        src = packed.at[0] if part is None else packed.at[0, part]
-        remote(src, dst, relay_s.at[k, s], recv.at[k, s], me).wait_recv()
-
     def relay(k, s):
-        to = me + 4 if k == 1 else me - 4
+        to = me + 8 * k - 4
         return remote(A.at[k, s], A.at[1 - k, s], relay_s.at[k, s], recv.at[1 - k, s], to)
 
-    last = {0: q == 0, 1: q == nq - 1}
-
-    def first_stop(k, s):
-        @pl.when(last[k])
-        def _():
-            arrived(k, s, half[k])
-
-        @pl.when(jnp.logical_not(last[k]))
-        def _():
-            arrived(k, s)
-            relay(k, s).start()
-
-        forward(k, s)
-
-    def second_stop(k, s):
-        arrived(k, s)
-        forward(k, s)
-
-    def source(kind, k, d):
-        below = (kind == "first") == (k == 1)
-        s = q - d if below else q + d
-        return s, (s >= 0 if below else s < nq)
-
-    items = []
-    order = [("first", 1), ("second", 1)]
-    order += [("first", d) for d in range(2, nq)] + [("second", d) for d in range(2, nq)]
-    for kind, d in order:
-        for k in (1, 0):
-            items.append((kind, k, d))
-
-    for copy in selfs:
-        copy.wait()
-    for k in (0, 1):
-        forward(k, q)
-
-    def diag_item(item):
-        kind, k, d = item
-        s, ok = source(kind, k, d)
-
-        @pl.when(ok)
-        def _():
-            diag_forward(k, s)
-
-    lag = 4
-    for t, (kind, k, d) in enumerate(items):
-        s, ok = source(kind, k, d)
-
-        @pl.when(ok)
-        def _(kind=kind, k=k, s=s):
-            (first_stop if kind == "first" else second_stop)(k, s)
-
-        if t == 1:
-            for kk in (0, 1):
-                diag_forward(kk, q)
-        if t >= lag:
-            diag_item(items[t - lag])
-    for item in items[max(0, len(items) - lag):]:
-        diag_item(item)
+    def item(t):
+        v = jnp.maximum(t - 2, 0)
+        j = jnp.where(t < 2, 0, 1 + lax.rem(v, nq - 1))
+        e = jnp.where(t < 2, t, v // (nq - 1))
+        m = jnp.minimum(q, nq - 1 - q)
+        d = (j + 1) // 2
+        near = jnp.where(lax.rem(j, 2) == 1, q - d, q + d)
+        far = jnp.where(q > nq - 1 - q, q - (j - m), q + (j - m))
+        s = jnp.where(j <= 2 * m, near, far)
+        return jnp.where(s < q, 1 - e, e), s, e
+
+    def edge(k):
+        return jnp.logical_or(
+            jnp.logical_and(k == 1, q == nq - 1), jnp.logical_and(k == 0, q == 0)
+        )
+
+    def relays(k, s, e):
+        return jnp.logical_and(
+            jnp.logical_and(e == 0, s != q), jnp.logical_not(edge(k))
+        )
 
     for p in range(4):
-        qid[p, 0:1, :] = jnp.concatenate([IDS[4 * s + p, 2:3, :] for s in range(nq)], axis=1)
+        for s in range(nq):
+            for k in (0, 1):
+                qid[2 * s + k, 0:1, cr * p : cr * (p + 1)] = IDS[
+                    4 * s + p, 2:3, cr * k : cr * (k + 1)
+                ]
     row = jnp.concatenate([IDS[4 * s + r, k : k + 1, :] for k in (0, 1) for s in range(nq)], axis=1)
     colid[...] = jnp.broadcast_to(row, (128, 2 * rows)).T.reshape(colid.shape)
     racc[...] = jnp.full(racc.shape, FILL, F32)
     cacc[...] = jnp.full(cacc.shape, FILL, F32)
 
-    @pl.loop(0, nq)
-    def _(s):
-        for k in (0, 1):
-            parts(k, s)[2].wait()
+    lane = lax.broadcasted_iota(jnp.int32, (cr2, 128), 1)
+    sub = lax.broadcasted_iota(jnp.int32, (cr2, 128), 0)
+
+    def tile(ta, tb):
+        k, s, _ = item(ta)
+        kb, sb, _ = item(tb)
+        ks, at_b = k * nq + s, 2 * sb + kb
+        scores = nt(A[k, s], Q[sb, kb].reshape(4 * cr, Q.shape[-1]))
+        off = cr * (1 - k)
+        own = jnp.logical_and(sub >= off, sub < off + cr)
+        base = jnp.where(ta == tb, r * cr - off, -4 * rows)
+        twin = jnp.where(own, sub + base, -1) - lane
+        col = colid[ks]
+        acc = racc[ks]
+        for j in range(4 * cr // 128):
+            at = slice(128 * j, 128 * (j + 1))
+            keep = jnp.logical_and(col == qid[at_b, 0:1, at], twin != 128 * j)
+            block = jnp.where(keep, scores[:, at], FILL)
+            acc = jnp.maximum(acc, block)
+            cacc[at_b, 0:1, at] = jnp.maximum(
+                cacc[at_b, 0:1, at], jnp.max(block, axis=0, keepdims=True)
+            )
+        racc[ks] = acc
+
+    for copy in selfs:
+        copy.wait()
+
+    @pl.loop(0, 2 * nq + 1)
+    def _(t):
+        @pl.when(t < 2 * nq)
+        def _():
+            k, s, e = item(t)
+
+            @pl.when(s != q)
+            def _():
+                @pl.when(edge(k))
+                def _():
+                    remote(
+                        packed.at[0, half(k)], mine(k, s), relay_s.at[k, s], recv.at[k, s], me
+                    ).wait_recv()
+
+                @pl.when(jnp.logical_not(edge(k)))
+                def _():
+                    remote(
+                        packed.at[0], A.at[k, s], relay_s.at[k, s], recv.at[k, s], me
+                    ).wait_recv()
+
+            @pl.when(relays(k, s, e))
+            def _():
+                relay(k, s).start()
+
+            forward(k, s)
+
+        @pl.when(t > 0)
+        def _():
+            k, s, _ = item(t - 1)
+            own_copy(k, s).wait()
             c_in(k, s).wait_recv()
             d_in(k, s).wait_recv()
 
-    lane = lax.broadcasted_iota(jnp.int32, (cr2, 128), 1)
-    sub = lax.broadcasted_iota(jnp.int32, (cr2, 128), 0)
-
-    @pl.loop(0, 8 * nq)
-    def _(step):
-        p = step // (2 * nq)
-        ks = lax.rem(step, 2 * nq)
-        k, s = ks // nq, lax.rem(ks, nq)
-        right = Q[p].reshape(rows, Q.shape[-1])
-        scores = nt(A[k, s], right)
-        col = colid[ks]
-        own = jnp.where(k == 0, jnp.where(sub >= cr, 1, 0), jnp.where(sub < cr, 1, 0))
-        own = jnp.where(p == r, own, 0)
-        twin = jnp.where(own == 1, s * cr2 + sub + jnp.where(k == 0, -cr, cr), -1) - lane
-        acc = racc[ks]
-        for j in range(rows // 128):
-            at = slice(128 * j, 128 * (j + 1))
-            keep = jnp.logical_and(col == qid[p, 0:1, at], twin != 128 * j)
-            block = jnp.where(keep, scores[:, at], FILL)
-            acc = jnp.maximum(acc, block)
-            cacc[p, 0:1, at] = jnp.maximum(cacc[p, 0:1, at], jnp.max(block, axis=0, keepdims=True))
-        racc[ks] = acc
+            @pl.loop(0, t)
+            def _(u):
+                tile(u, t - 1)
+
+        @pl.when(t < 2 * nq)
+        def _():
+            k, s, _ = item(t)
+            y_in(k, s).wait_recv()
+            diag(k, s).start()
+
+            @pl.loop(0, t)
+            def _(u):
+                tile(t, u)
 
     best = jnp.max(racc[...].reshape(2 * rows, 128).T, axis=0, keepdims=True)
     fill = jnp.full((1, cr2), FILL, F32)
@@ -297,7 +311,9 @@
             for k in (0, 1):
                 at = (k * nq + s) * cr2
                 MSG[to, k : k + 1, :] = jnp.where(same, best[:, at : at + cr2], fill)
-            MSG[to, 2:3, :] = cacc[p, 0:1, cr2 * s : cr2 * (s + 1)]
+            MSG[to, 2:3, :] = jnp.concatenate(
+                [cacc[2 * s + k, 0:1, cr * p : cr * (p + 1)] for k in (0, 1)], axis=1
+            )
             MSG[to, 3:8, :] = jnp.zeros((5, cr2), F32)
 
     def msg_copy(o):
@@ -318,21 +334,16 @@
     def _(o):
         ids_copy(o).wait_send()
 
-    @pl.loop(0, nq)
-    def _(s):
-        for k in (0, 1):
-            y, c, _ = parts(k, s)
-            y.wait_send()
-            c.wait_send()
-            diag(k, s).wait_send()
-
-    for kind, k, d in items:
-        if kind == "first":
-            s, ok = source(kind, k, d)
-
-            @pl.when(jnp.logical_and(ok, jnp.logical_not(last[k])))
-            def _(k=k, s=s):
-                relay(k, s).wait_send()
+    @pl.loop(0, 2 * nq)
+    def _(t):
+        k, s, e = item(t)
+        y_copy(k, s).wait_send()
+        c_copy(k, s).wait_send()
+        diag(k, s).wait_send()
+
+        @pl.when(relays(k, s, e))
+        def _():
+            relay(k, s).wait_send()
 
     key = key_ref[...]
     bits = cr2.bit_length() - 1
@@ -400,14 +411,14 @@
         out_specs=vmem,
         scratch_shapes=[
             pltpu.VMEM((2, nq, 2 * cr, width), BF16),
-            pltpu.VMEM((4, nq, 2 * cr, width), BF16),
+            pltpu.VMEM((nq, 2, 4, cr, width), BF16),
             pltpu.VMEM((n, 8, 2 * cr), jnp.int32),
             pltpu.VMEM((n, 8, 2 * cr), F32),
             pltpu.VMEM((n, 8, 2 * cr), F32),
             pltpu.VMEM((2 * nq, 2 * cr, 128), F32),
-            pltpu.VMEM((4, 8, rows), F32),
+            pltpu.VMEM((2 * nq, 8, 4 * cr), F32),
             pltpu.VMEM((2 * nq, 2 * cr, 128), jnp.int32),
-            pltpu.VMEM((4, 8, rows), jnp.int32),
+            pltpu.VMEM((2 * nq, 8, 4 * cr), jnp.int32),
             dma((nq + 1,)),
             dma((2, nq)), dma((2, nq)), dma((2, nq)), dma((2, nq)),
             dma((2, nq)), dma((2, nq)), dma((2, nq)), dma((2, nq)),

time: 98.5 us -> 90.5 us (0.919)
  Pallas kernels: 94.8 us -> 86.8 us
    pallas_call x1, Pallas kernels: 92.1 us -> 84.1 us  [body(): pl.pallas_call(functools.partial(main_kernel, n), out_shape=jax.ShapeDtyp...]
where the time goes in v2:
time: 90.5 us; the launch traced here: 90.2 us
  Pallas kernels  86.8 us (96%)
  local copies, waits for them, and re-layouts  3.38 us (4%)
    pallas_call x1, Pallas kernels, body(): pl.pallas_call(functools.partial(main_kernel, n), out_shape=jax.ShapeDtyp...  84.1 us
    unnamed x7, local copies, waits for them, and re-layouts  3.38 us
    pallas_call x1, Pallas kernels, body(): pl.pallas_call(functools.partial(pack_kernel, n), out_shape=(jax.ShapeDty...  2.72 us

profile of v2, /device:TPU:0, one launch (start us, length us, event | category | flops | bytes accessed | tf_op | source)
XLA Modules:
  0.0 90.2 jit_solution(7318115518516422647)
XLA Ops:
  0.0 0.0 copy-start
  0.0 1.4 %copy-done = bf16[1024,768]{1,0:T(8,128)(2,1)S(1)} copy-done((bf16[1024,768]{1,0:T(8,128)(2,1)S(1)}, bf16[1024,768]{1,0:T(8,128)(2,1)}, u32[]{:S(2)}) %copy-start) | copy-done | bytes 1572888
  1.4 0.0 copy-start.1
  1.4 0.7 copy-done.1
  2.1 0.0 copy-start.2
  2.1 0.7 copy-done.2
  2.8 2.7 %shard_map.37 = (bf16[1280,768]{1,0:T(8,128)(2,1)S(1)}, s32[4,8,256]{2,1,0:T(8,128)S(1)}, s32[1,1024]{1,0:T(1,128)S(1)}) custom-call(bf16[1024,768]{1,0:T(8,128)(2,1)S(1)} %copy-done, s32[1,1024]{1,0:T(1,128)S(1)} %bitcast.6, s32[1,1024]{1,0:T(1,128)S(1)} %bitcast.7), custom_call_target="tpu_custom_call" | custom-call | tf_op jit(solution)/shard_map/pallas_call | solution.py:395
  5.5 84.1 %shard_map.38 = f32[1,1024]{1,0:T(1,128)S(1)} custom-call(bf16[5,256,768]{2,1,0:T(8,128)(2,1)S(1)} %bitcast.4, s32[4,8,256]{2,1,0:T(8,128)S(1)} %get-tuple-element.9.idm, s32[1,1024]{1,0:T(1,128)S(1)} %get-tuple-element.10.key_ref), custom_call_target="tpu_custom_call" | custom-call | tf_op jit(solution)/shard_map/pallas_call | solution.py:407
  89.6 0.6 copy.5
Async XLA Ops:
  0.0 1.4 %copy-start = (bf16[1024,768]{1,0:T(8,128)(2,1)S(1)}, bf16[1024,768]{1,0:T(8,128)(2,1)}, u32[]{:S(2)}) copy-start(bf16[1024,768]{1,0:T(8,128)(2,1)} %emb.1) | copy-start | bytes 4718596
  1.4 0.7 copy-start.1
  2.1 0.7 copy-start.2

commit v3 on v2

--- a/solution.py
+++ b/solution.py
@@ -45,10 +45,9 @@
     none = jnp.full((1, cr), -1, jnp.int32)
     padded = jnp.concatenate([none, ids, none], axis=1)
     for q in range(nq):
-        idm[q, 0:1, :] = padded[:, 2 * cr * q : 2 * cr * (q + 1)]
-        idm[q, 1:2, :] = padded[:, 2 * cr * (q + 1) : 2 * cr * (q + 2)]
-        idm[q, 2:3, :] = ids[:, 2 * cr * q : 2 * cr * (q + 1)]
-        idm[q, 3:8, :] = jnp.zeros((5, 2 * cr), jnp.int32)
+        idm[q] = jnp.concatenate(
+            [padded[:, 2 * cr * q : 2 * cr * (q + 2)], ids[:, 2 * cr * q : 2 * cr * (q + 1)]], axis=1
+        )
 
 
 def pick(table, hot):
@@ -221,9 +220,9 @@
         for s in range(nq):
             for k in (0, 1):
                 qid[2 * s + k, 0:1, cr * p : cr * (p + 1)] = IDS[
-                    4 * s + p, 2:3, cr * k : cr * (k + 1)
+                    4 * s + p, :, 2 * cr2 + cr * k : 2 * cr2 + cr * (k + 1)
                 ]
-    row = jnp.concatenate([IDS[4 * s + r, k : k + 1, :] for k in (0, 1) for s in range(nq)], axis=1)
+    row = jnp.concatenate([IDS[4 * s + r, :, k * cr2 : (k + 1) * cr2] for k in (0, 1) for s in range(nq)], axis=1)
     colid[...] = jnp.broadcast_to(row, (128, 2 * rows)).T.reshape(colid.shape)
     racc[...] = jnp.full(racc.shape, FILL, F32)
     cacc[...] = jnp.full(cacc.shape, FILL, F32)
@@ -255,7 +254,7 @@
     for copy in selfs:
         copy.wait()
 
-    @pl.loop(0, 2 * nq + 1)
+    @pl.loop(0, 2 * nq + 2)
     def _(t):
         @pl.when(t < 2 * nq)
         def _():
@@ -281,24 +280,26 @@
 
             forward(k, s)
 
-        @pl.when(t > 0)
+        @pl.when(jnp.logical_and(t >= 1, t < 2 * nq + 1))
         def _():
             k, s, _ = item(t - 1)
+            y_in(k, s).wait_recv()
+            diag(k, s).start()
+
+        @pl.when(t >= 2)
+        def _():
+            k, s, _ = item(t - 2)
             own_copy(k, s).wait()
             c_in(k, s).wait_recv()
             d_in(k, s).wait_recv()
 
-            @pl.loop(0, t)
+            @pl.loop(0, jnp.minimum(t + 1, 2 * nq))
             def _(u):
-                tile(u, t - 1)
-
-        @pl.when(t < 2 * nq)
+                tile(u, t - 2)
+
+        @pl.when(jnp.logical_and(t >= 3, t < 2 * nq))
         def _():
-            k, s, _ = item(t)
-            y_in(k, s).wait_recv()
-            diag(k, s).start()
-
-            @pl.loop(0, t)
+            @pl.loop(0, t - 2)
             def _(u):
                 tile(t, u)
 
@@ -308,13 +309,10 @@
         for p in range(4):
             to = 4 * s + p
             same = p == r
-            for k in (0, 1):
-                at = (k * nq + s) * cr2
-                MSG[to, k : k + 1, :] = jnp.where(same, best[:, at : at + cr2], fill)
-            MSG[to, 2:3, :] = jnp.concatenate(
-                [cacc[2 * s + k, 0:1, cr * p : cr * (p + 1)] for k in (0, 1)], axis=1
-            )
-            MSG[to, 3:8, :] = jnp.zeros((5, cr2), F32)
+            found = [best[:, (k * nq + s) * cr2 : (k * nq + s + 1) * cr2] for k in (0, 1)]
+            found = [jnp.where(same, one, fill) for one in found]
+            found += [cacc[2 * s + k, 0:1, cr * p : cr * (p + 1)] for k in (0, 1)]
+            MSG[to] = jnp.concatenate(found, axis=1)
 
     def msg_copy(o):
         to = lax.rem(me + o, n)
@@ -359,9 +357,9 @@
         remote(MSG.at[0], MSGR.at[frm], msg_s.at[o], msg_r.at[frm], frm).wait_recv()
 
     def top(s, k):
-        found = MSGR[4 * s, k : k + 1, :]
+        found = MSGR[4 * s, :, k * cr2 : (k + 1) * cr2]
         for p in range(1, 4):
-            found = jnp.maximum(found, MSGR[4 * s + p, k : k + 1, :])
+            found = jnp.maximum(found, MSGR[4 * s + p, :, k * cr2 : (k + 1) * cr2])
         return found
 
     segs = []
@@ -396,7 +394,7 @@
         functools.partial(pack_kernel, n),
         out_shape=(
             jax.ShapeDtypeStruct((rows + 2 * cr, width), BF16),
-            jax.ShapeDtypeStruct((nq, 8, 2 * cr), jnp.int32),
+            jax.ShapeDtypeStruct((nq, 1, 6 * cr), jnp.int32),
             jax.ShapeDtypeStruct((1, rows), jnp.int32),
         ),
         in_specs=[vmem] * 3,
@@ -412,9 +410,9 @@
         scratch_shapes=[
             pltpu.VMEM((2, nq, 2 * cr, width), BF16),
             pltpu.VMEM((nq, 2, 4, cr, width), BF16),
-            pltpu.VMEM((n, 8, 2 * cr), jnp.int32),
-            pltpu.VMEM((n, 8, 2 * cr), F32),
-            pltpu.VMEM((n, 8, 2 * cr), F32),
+            pltpu.VMEM((n, 1, 6 * cr), jnp.int32),
+            pltpu.VMEM((n, 1, 6 * cr), F32),
+            pltpu.VMEM((n, 1, 6 * cr), F32),
             pltpu.VMEM((2 * nq, 2 * cr, 128), F32),
             pltpu.VMEM((2 * nq, 8, 4 * cr), F32),
             pltpu.VMEM((2 * nq, 2 * cr, 128), jnp.int32),

time: 90.5 us -> 81.2 us (0.90)
  Pallas kernels: 86.8 us -> 77.5 us
    pallas_call x1, Pallas kernels: 84.1 us -> 74.8 us  [body(): pl.pallas_call(functools.partial(main_kernel, n), out_shape=jax.ShapeDtyp...]
where the time goes in v3:
time: 81.2 us; the launch traced here: 80.9 us
  Pallas kernels  77.5 us (95%)
  local copies, waits for them, and re-layouts  3.38 us (4%)
    pallas_call x1, Pallas kernels, body(): pl.pallas_call(functools.partial(main_kernel, n), out_shape=jax.ShapeDtyp...  74.8 us
    unnamed x7, local copies, waits for them, and re-layouts  3.38 us
    pallas_call x1, Pallas kernels, body(): pl.pallas_call(functools.partial(pack_kernel, n), out_shape=(jax.ShapeDty...  2.77 us

profile of v3, /device:TPU:0, one launch (start us, length us, event | category | flops | bytes accessed | tf_op | source)
XLA Modules:
  0.0 80.9 jit_solution(15499417036674084488)
XLA Ops:
  0.0 0.0 copy-start
  0.0 1.4 %copy-done = bf16[1024,768]{1,0:T(8,128)(2,1)S(1)} copy-done((bf16[1024,768]{1,0:T(8,128)(2,1)S(1)}, bf16[1024,768]{1,0:T(8,128)(2,1)}, u32[]{:S(2)}) %copy-start) | copy-done | bytes 1572888
  1.4 0.0 copy-start.1
  1.4 0.7 copy-done.1
  2.1 0.0 copy-start.2
  2.1 0.7 copy-done.2
  2.8 2.8 %shard_map.37 = (bf16[1280,768]{1,0:T(8,128)(2,1)S(1)}, s32[4,1,768]{2,1,0:T(1,128)S(1)}, s32[1,1024]{1,0:T(1,128)S(1)}) custom-call(bf16[1024,768]{1,0:T(8,128)(2,1)S(1)} %copy-done, s32[1,1024]{1,0:T(1,128)S(1)} %bitcast.6, s32[1,1024]{1,0:T(1,128)S(1)} %bitcast.7), custom_call_target="tpu_custom_call" | custom-call | tf_op jit(solution)/shard_map/pallas_call | solution.py:393
  5.6 74.8 %shard_map.38 = f32[1,1024]{1,0:T(1,128)S(1)} custom-call(bf16[5,256,768]{2,1,0:T(8,128)(2,1)S(1)} %bitcast.4, s32[4,1,768]{2,1,0:T(1,128)S(1)} %get-tuple-element.9.idm, s32[1,1024]{1,0:T(1,128)S(1)} %get-tuple-element.10.key_ref), custom_call_target="tpu_custom_call" | custom-call | tf_op jit(solution)/shard_map/pallas_call | solution.py:405
  80.3 0.6 copy.5
Async XLA Ops:
  0.0 1.4 %copy-start = (bf16[1024,768]{1,0:T(8,128)(2,1)S(1)}, bf16[1024,768]{1,0:T(8,128)(2,1)}, u32[]{:S(2)}) copy-start(bf16[1024,768]{1,0:T(8,128)(2,1)} %emb.1) | copy-start | bytes 4718596
  1.4 0.7 copy-start.1
  2.1 0.7 copy-start.2

commit v4 on v3

--- a/solution.py
+++ b/solution.py
@@ -18,13 +18,18 @@
     return lax.dot_general(a, b, (((1,), (1,)), ((), ())), preferred_element_type=F32)
 
 
-def pack_kernel(n, emb, cl, tp, packed, idm, key_ref):
+def pack_kernel(n, emb_in, cl_in, tp_in, packed, idm, key_ref, emb, cl, tp, sem):
+    fetch = [
+        pltpu.make_async_copy(src, dst, sem.at[i])
+        for i, (src, dst) in enumerate(((tp_in, tp), (cl_in, cl), (emb_in, emb)))
+    ]
+    for copy in fetch:
+        copy.start()
     rows, width = emb.shape
     piece = rows // n
     nq, cr = n // 4, 2 * piece
     shift = rows.bit_length() - 1
-    x = emb[...].astype(F32)
-    unit = (x * lax.rsqrt(jnp.sum(x * x, axis=1, keepdims=True) + 1e-06)).astype(BF16)
+    fetch[0].wait()
     dest = lax.shift_right_logical(tp[...], shift)
     hit = lax.broadcasted_iota(jnp.int32, (n, rows), 0) == dest
     hot = jnp.where(hit, 1.0, 0.0)
@@ -37,9 +42,13 @@
     key_ref[...] = key
     perm = jnp.where(i0 == key, 1.0, 0.0).astype(BF16)
     zero = jnp.zeros((cr, width), BF16)
+    fetch[2].wait()
+    x = emb[...].astype(F32)
+    unit = (x * lax.rsqrt(jnp.sum(x * x, axis=1, keepdims=True) + 1e-06)).astype(BF16)
     packed[pl.ds(0, cr), :] = zero
     packed[pl.ds(cr, rows), :] = jnp.dot(perm, unit, preferred_element_type=F32).astype(BF16)
     packed[pl.ds(cr + rows, cr), :] = zero
+    fetch[1].wait()
     labels = jnp.broadcast_to(cl[...].astype(F32), (8, rows)).astype(BF16)
     ids = nt(labels, perm).astype(jnp.int32)[0:1]
     none = jnp.full((1, cr), -1, jnp.int32)
@@ -230,11 +239,15 @@
     lane = lax.broadcasted_iota(jnp.int32, (cr2, 128), 1)
     sub = lax.broadcasted_iota(jnp.int32, (cr2, 128), 0)
 
-    def tile(ta, tb):
+    def scores_of(ta, tb):
+        k, s, _ = item(ta)
+        kb, sb, _ = item(tb)
+        return nt(A[k, s], Q[sb, kb].reshape(4 * cr, Q.shape[-1]))
+
+    def take(ta, tb, scores):
         k, s, _ = item(ta)
         kb, sb, _ = item(tb)
         ks, at_b = k * nq + s, 2 * sb + kb
-        scores = nt(A[k, s], Q[sb, kb].reshape(4 * cr, Q.shape[-1]))
         off = cr * (1 - k)
         own = jnp.logical_and(sub >= off, sub < off + cr)
         base = jnp.where(ta == tb, r * cr - off, -4 * rows)
@@ -251,6 +264,14 @@
             )
         racc[ks] = acc
 
+    def tiles(count, pair):
+        @pl.loop(0, (count + 1) // 2)
+        def _(i):
+            one, two = pair(2 * i), pair(jnp.minimum(2 * i + 1, count - 1))
+            first, second = scores_of(*one), scores_of(*two)
+            take(*one, first)
+            take(*two, second)
+
     for copy in selfs:
         copy.wait()
 
@@ -293,15 +314,11 @@
             c_in(k, s).wait_recv()
             d_in(k, s).wait_recv()
 
-            @pl.loop(0, jnp.minimum(t + 1, 2 * nq))
-            def _(u):
-                tile(u, t - 2)
+            tiles(jnp.minimum(t + 1, 2 * nq), lambda u: (u, t - 2))
 
         @pl.when(jnp.logical_and(t >= 3, t < 2 * nq))
         def _():
-            @pl.loop(0, t - 2)
-            def _(u):
-                tile(t, u)
+            tiles(t - 2, lambda u: (t, u))
 
     best = jnp.max(racc[...].reshape(2 * rows, 128).T, axis=0, keepdims=True)
     fill = jnp.full((1, cr2), FILL, F32)
@@ -397,8 +414,14 @@
             jax.ShapeDtypeStruct((nq, 1, 6 * cr), jnp.int32),
             jax.ShapeDtypeStruct((1, rows), jnp.int32),
         ),
-        in_specs=[vmem] * 3,
+        in_specs=[pl.BlockSpec(memory_space=pl.ANY)] * 3,
         out_specs=(vmem,) * 3,
+        scratch_shapes=[
+            pltpu.VMEM((rows, width), BF16),
+            pltpu.VMEM((1, rows), jnp.int32),
+            pltpu.VMEM((1, rows), jnp.int32),
+            pltpu.SemaphoreType.DMA((3,)),
+        ],
         compiler_params=pltpu.CompilerParams(vmem_limit_bytes=40 * 2**20),
     )(embeddings, cluster_of.reshape(1, rows), target_pos.reshape(1, rows))
     dma = pltpu.SemaphoreType.DMA

time: 81.2 us -> 79.6 us (0.980)
  Pallas kernels: 77.5 us -> 76 us
    pallas_call x1, Pallas kernels: 74.8 us -> 71.2 us  [body(): pl.pallas_call(functools.partial(main_kernel, n), out_shape=jax.ShapeDtyp...]
    pallas_call x1, Pallas kernels: 2.77 us -> 4.73 us  [body(): pl.pallas_call(functools.partial(pack_kernel, n), out_shape=(jax.ShapeDty...]
where the time goes in v4:
time: 79.6 us; the launch traced here: 79.4 us
  Pallas kernels  76 us (95%)
  local copies, waits for them, and re-layouts  3.38 us (4%)
    pallas_call x1, Pallas kernels, body(): pl.pallas_call(functools.partial(main_kernel, n), out_shape=jax.ShapeDtyp...  71.2 us
    pallas_call x1, Pallas kernels, body(): pl.pallas_call(functools.partial(pack_kernel, n), out_shape=(jax.ShapeDty...  4.73 us
    unnamed x7, local copies, waits for them, and re-layouts  3.38 us

profile of v4, /device:TPU:0, one launch (start us, length us, event | category | flops | bytes accessed | tf_op | source)
XLA Modules:
  0.0 79.4 jit_solution(586674113753524903)
XLA Ops:
  0.0 0.0 copy-start
  0.0 1.4 %copy-done = bf16[1024,768]{1,0:T(8,128)(2,1)S(1)} copy-done((bf16[1024,768]{1,0:T(8,128)(2,1)S(1)}, bf16[1024,768]{1,0:T(8,128)(2,1)}, u32[]{:S(2)}) %copy-start) | copy-done | bytes 1572888
  1.4 0.0 copy-start.1
  1.4 0.7 copy-done.1
  2.1 0.0 copy-start.2
  2.1 0.7 copy-done.2
  2.8 4.7 %shard_map.37 = (bf16[1280,768]{1,0:T(8,128)(2,1)S(1)}, s32[4,1,768]{2,1,0:T(1,128)S(1)}, s32[1,1024]{1,0:T(1,128)S(1)}) custom-call(bf16[1024,768]{1,0:T(8,128)(2,1)S(1)} %copy-done, s32[1,1024]{1,0:T(1,128)S(1)} %bitcast.6, s32[1,1024]{1,0:T(1,128)S(1)} %bitcast.7), custom_call_target="tpu_custom_call" | custom-call | tf_op jit(solution)/shard_map/pallas_call | solution.py:410
  7.5 71.2 %shard_map.38 = f32[1,1024]{1,0:T(1,128)S(1)} custom-call(bf16[5,256,768]{2,1,0:T(8,128)(2,1)S(1)} %bitcast.4, s32[4,1,768]{2,1,0:T(1,128)S(1)} %get-tuple-element.9.idm, s32[1,1024]{1,0:T(1,128)S(1)} %get-tuple-element.10.key_ref), custom_call_target="tpu_custom_call" | custom-call | tf_op jit(solution)/shard_map/pallas_call | solution.py:428
  78.8 0.6 copy.5
Async XLA Ops:
  0.0 1.4 %copy-start = (bf16[1024,768]{1,0:T(8,128)(2,1)S(1)}, bf16[1024,768]{1,0:T(8,128)(2,1)}, u32[]{:S(2)}) copy-start(bf16[1024,768]{1,0:T(8,128)(2,1)} %emb_in.1) | copy-start | bytes 4718596
  1.4 0.7 copy-start.1
  2.1 0.7 copy-start.2
